TPU v7x, 32 devices: a whole 2x2x4 slice. The times are simulated.
32 devices in a mesh: groups: 2 (over y), space: 16 (over z, x, core).
Axes of the slice: x: 2, y: 2, z: 4, core: 2. Of those that a mesh axis runs over, the one named last changes fastest.
Arguments:
- modes: float32 [4, 128, 32, 64], P('groups', None, 'space'), parts along dimension 0, may hold values from -6 to 6
- cell_weight: float32 [32, 128], P('space', 'groups'), parts along dimension 1, may hold values from 0.5 to 2
- seeds: int32 [256], P(('groups', 'space')), parts along dimension 0, may hold values from 0 to 255
- coeff_table: float32 [256, 128], replicated, may hold values from -6 to 6
- force_table: float32 [256, 128], replicated, may hold values from -6 to 6
- visc_table: float32 [256], replicated, may hold values from 0.02 to 0.2
Outputs:
- coefficients: float32 [256, 128], P(('groups', 'space')), parts along dimension 0
There are 2 independent parts, one for each index of `groups`. A program takes and returns all parts, laid end to end along the dimension named above; an argument that names none is the same for every part. Nothing has to cross between parts.
All inputs are finite; a program needn't handle non-finite values.
Results may differ from a plain program's by a relative error of at most 0.00013.
Values sent between devices are 32-bit elements; how exact they have to be, the bound alone decides.
A program may use at most 64 MiB of HBM per device.

v0:
```python
import math
import jax
import jax.numpy as jnp
from jax import lax
from jax.sharding import PartitionSpec as P

STEPS = 2
TIME_STEP = 0.5


def padded_2(array, sides, width):
    for axis, dim in sides:
        devices, length = (lax.axis_size(axis), array.shape[dim])
        up = [(i, (i + 1) % devices) for i in range(devices)]
        down = [(j, i) for i, j in up]
        last = lax.slice_in_dim(array, length - width, length, axis=dim)
        first = lax.slice_in_dim(array, 0, width, axis=dim)
        before = lax.ppermute(last, axis, up)
        after = lax.ppermute(first, axis, down)
        array = jnp.concatenate([before, array, after], axis=dim)
    return array


def shards(modes, cell_weight, seeds, coeff_table, force_table, visc_table):
    mode_count = modes.shape[1]
    slab_cells = modes.shape[2]
    across = modes.shape[3]
    devices = lax.axis_size("space")
    cell_count = slab_cells * across
    total_cells = cell_count * devices
    padded = padded_2(modes, (("space", 2),), 2)
    slope_along = (
        padded[:, :, 0:slab_cells]
        - 8.0 * padded[:, :, 1 : slab_cells + 1]
        + 8.0 * padded[:, :, 3 : slab_cells + 3]
        - padded[:, :, 4 : slab_cells + 4]
    ) / 12.0
    slope_across = (
        jnp.roll(modes, 2, 3)
        - 8.0 * jnp.roll(modes, 1, 3)
        + 8.0 * jnp.roll(modes, -1, 3)
        - jnp.roll(modes, -2, 3)
    ) / 12.0
    slopes = jnp.stack([slope_along, slope_across]).reshape(2, 2, mode_count, cell_count)
    velocity = modes.reshape(2, mode_count, cell_count)
    cell_scale = cell_weight.reshape(cell_count) / total_cells
    weighted = velocity * cell_scale[None, None, :]
    diffusion = lax.psum(
        jnp.einsum(
            "taic,tajc->ij",
            slopes * cell_scale[None, None, None, :],
            slopes,
            precision=lax.Precision.HIGHEST,
        ),
        "space",
    )
    selector = (
        seeds[:, None] == jnp.arange(coeff_table.shape[0], dtype=jnp.int32)[None, :]
    ).astype(jnp.float32)
    coeffs = jnp.dot(selector, coeff_table, precision=lax.Precision.HIGHEST)
    forcing = jnp.dot(selector, force_table, precision=lax.Precision.HIGHEST)
    viscosity = jnp.dot(selector, visc_table, precision=lax.Precision.HIGHEST)
    own_count = coeffs.shape[0]

    def field_block(coeff_rows):
        flow = jnp.einsum("ni,aic->anc", coeff_rows, velocity, precision=lax.Precision.HIGHEST)
        grads = jnp.einsum("nk,takc->tanc", coeff_rows, slopes, precision=lax.Precision.HIGHEST)
        carried = jnp.sum(flow[:, None, :, :] * grads, axis=0)
        return jnp.einsum("aic,anc->ni", weighted, carried, precision=lax.Precision.HIGHEST)

    for repeat in range(STEPS):
        everyone = lax.all_gather(coeffs, "space", axis=0, tiled=True)
        rows_each = math.gcd(own_count * lax.axis_size("space"), 128)
        stacked = everyone.reshape(
            own_count * lax.axis_size("space") // rows_each, rows_each, mode_count
        )
        quadratic = lax.psum_scatter(
            lax.map(field_block, stacked).reshape(own_count * lax.axis_size("space"), mode_count),
            "space",
            scatter_dimension=0,
            tiled=True,
        )
        linear = jnp.dot(coeffs, diffusion, precision=lax.Precision.HIGHEST)
        coeffs = coeffs + TIME_STEP * (forcing - viscosity[:, None] * linear - quadratic)
    return coeffs


def solution(mesh):
    placed = (
        P("groups", None, "space", None),
        P("space", "groups"),
        P(("groups", "space")),
        P(),
        P(),
        P(),
    )
    return jax.shard_map(
        shards, mesh=mesh, in_specs=placed, out_specs=P(("groups", "space"), None), check_vma=False
    )
```

profile of v0, /device:TPU:8, one launch (start us, length us, event | category | flops | bytes accessed | tf_op | source)
XLA Modules:
  0.0 243.6 jit_solution(18027088971304564999)
XLA Ops:
  6.6 2.6 %collective-permute-start.1 = (f32[2,128,2,64]{1,3,2,0:T(8,128)}, f32[2,128,2,64]{1,3,2,0:T(8,128)S(1)}, u32[]{:S(2)}, u32[]{:S(2)}) collective-permute-start(f32[2,128,2,64]{1,3,2,0:T(8,128)} %param.6), channel_id=1, source_target_pairs={{1,0},{2,1},{3,2},{4,3},{5,4},{6,5},{7,6},{8,7},{9,8},{10,9},{11,1... | collective-permute-start | bytes 393224 | tf_op jit(solution)/shard_map/ppermute | solution.py:19
  9.2 1.0 slice_bitcast_fusion
  10.3 0.1 copy.35
  10.4 0.5 copy-done.4
  11.0 0.2 fusion.34
  11.2 18.1 %all_gather.6 = f32[128,128]{1,0:T(8,128)S(1)} all-gather(f32[8,128]{1,0:T(8,128)S(1)} %fusion.34), channel_id=1, replica_groups=mesh['groups'=2,'space'=16] {'space'}, dimensions={0}, use_global_device_ids=true | all-gather | bytes 69632 | tf_op jit(solution)/shard_map/all_gather | solution.py:72
  29.3 0.3 convolution_bitcast_fusion.3
  29.8 0.6 copy-done.5
  30.4 0.7 copy-done.7
  31.1 0.6 dynamic-slice.2
  32.3 0.2 fusion.33
  32.6 0.6 fusion.2
  33.2 1.0 convolution_bitcast_fusion.6
  34.3 1.0 convolution_bitcast_fusion.5
  35.4 0.6 copy-done.6
  36.0 0.2 convolution_bitcast_fusion.7
  36.2 90.3 %all-reduce.8.cloned.1.call-done = (f32[128,128]{1,0:T(8,128)}, f32[128,128]{1,0:T(8,128)}) async-done(((f32[128,128]{1,0:T(8,128)}, f32[128,128]{1,0:T(8,128)}), (f32[128,128]{1,0:T(8,128)}, f32[128,128]{1,0:T(8,128)})) %all-reduce.8.cloned.1.call-update) | async-done | bytes 131088 | tf_op jit(solution)/shard_map/psum | solution.py:48
  126.5 1.0 fusion.11
  127.4 16.9 %all_gather.7 = f32[128,128]{1,0:T(8,128)S(1)} all-gather(f32[8,128]{1,0:T(8,128)S(1)} %fusion.11), channel_id=1, replica_groups=mesh['groups'=2,'space'=16] {'space'}, dimensions={0}, use_global_device_ids=true | all-gather | bytes 69632 | tf_op jit(solution)/shard_map/all_gather | solution.py:72
  144.4 0.3 convolution_bitcast_fusion.2
  144.8 0.6 fusion.3
  145.4 1.0 convolution_bitcast_fusion.4
  146.4 88.9 %all-reduce.6.cloned.1.call-done = f32[128,128]{1,0:T(8,128)} async-done(((f32[128,128]{1,0:T(8,128)}), f32[128,128]{1,0:T(8,128)}) %all-reduce.6.cloned.1.call-update) | async-done | bytes 65552
  235.3 1.4 fusion.7
  (30 shorter events, 0.7 us)
Async XLA Ops:
  6.5 3.9 %copy-start = (f32[256,128]{1,0:T(8,128)S(1)}, f32[256,128]{1,0:T(8,128)}, u32[]{:S(2)}) copy-start(f32[256,128]{1,0:T(8,128)} %param.9) | copy-start | bytes 393220
  6.5 3.6 %copy-start.1 = (f32[2,128,2,64]{1,3,2,0:T(8,128)S(1)}, f32[2,128,2,64]{1,3,2,0:T(8,128)}, u32[]{:S(2)}) copy-start(f32[2,128,2,64]{1,3,2,0:T(8,128)} %param.6) | copy-start | bytes 393220
  6.5 119.9 %all-reduce.8.cloned.1.call-start = ((), (), s32[]{:S(2)}) async-start(), calls=%async_computation.1 | async-start | bytes 262144 | tf_op jit(solution)/shard_map/psum | solution.py:48
  6.5 26.0 %collective-permute-start = (f32[2,128,2,64]{1,3,2,0:T(8,128)}, f32[2,128,2,64]{1,3,2,0:T(8,128)S(1)}, u32[]{:S(2)}, u32[]{:S(2)}) collective-permute-start(f32[2,128,2,64]{1,3,2,0:T(8,128)} %param.6), channel_id=1, source_target_pairs={{0,1},{1,2},{2,3},{3,4},{4,5},{5,6},{6,7},{7,8},{8,9},{9,10},{10,1... | collective-permute-start | bytes 393224 | tf_op jit(solution)/shard_map/ppermute | solution.py:18
  6.6 25.9 %collective-permute-start.1 = (f32[2,128,2,64]{1,3,2,0:T(8,128)}, f32[2,128,2,64]{1,3,2,0:T(8,128)S(1)}, u32[]{:S(2)}, u32[]{:S(2)}) collective-permute-start(f32[2,128,2,64]{1,3,2,0:T(8,128)} %param.6), channel_id=1, source_target_pairs={{1,0},{2,1},{3,2},{4,3},{5,4},{6,5},{7,6},{8,7},{9,8},{10,9},{11,1... | collective-permute-start | bytes 393224 | tf_op jit(solution)/shard_map/ppermute | solution.py:19
  10.3 0.7 copy-start.4
  29.6 0.7 copy-start.5
  29.6 2.7 %copy-start.3 = (f32[256,128]{1,0:T(8,128)S(1)}, f32[256,128]{1,0:T(8,128)}, u32[]{:S(2)}) copy-start(f32[256,128]{1,0:T(8,128)} %param.10) | copy-start | bytes 393220
  30.4 0.7 copy-start.7
  35.3 0.7 copy-start.6
  35.3 200.0 %all-reduce.6.cloned.1.call-start = ((), (), s32[]{:S(2)}) async-start(), calls=%async_computation | async-start | bytes 131072
  146.4 88.9 %copy-start.2 = (f32[128,128]{1,0:T(8,128)S(1)}, f32[128,128]{1,0:T(8,128)}, u32[]{:S(2)}) copy-start(f32[128,128]{1,0:T(8,128)} %get-tuple-element.27) | copy-start | bytes 196612
Sparse Core Ops, SparseCore 0:
  35.4 90.9 all-reduce.7
  146.5 88.7 all-reduce.5
where the time goes:
time: 244 us
  waiting for transfers between devices  179 us (73%)
  blocking collectives  35 us (14%)
  between operations  14.2 us (6%)
  matrix products  7.78 us (3%)
  local copies, waits for them, and re-layouts  4.56 us (2%)
  starting transfers between devices  2.68 us (1%)
    psum x1, waiting for transfers between devices, shards(): lax.psum(jnp.einsum('taic,tajc->ij', slopes * cell_scale[None, None, None...  90.3 us
    unnamed x3, waiting for transfers between devices  88.9 us
    all_gather x2, blocking collectives, shards(): everyone = lax.all_gather(coeffs, 'space', axis=0, tiled=True)  35 us
  transfers between devices with their start and end apart: 4, of which 2 were waited for; matrix products, arithmetic and copies ran while one was open for 1% of the time, Pallas kernels for 0%

commit v1 on v0

--- a/solution.py
+++ b/solution.py
@@ -6,6 +6,33 @@
 
 STEPS = 2
 TIME_STEP = 0.5
+
+
+def extend_units_in(x_part, axis_no):
+    x_part = jnp.moveaxis(x_part, 0, axis_no)
+    passed = x_part.shape
+    return x_part.reshape(
+        *passed[:axis_no], passed[axis_no] * passed[axis_no + 1], *passed[axis_no + 2 :]
+    )
+
+
+def open_notes(block_in, mesh_ax):
+    extra = lax.psum(1, axis_name=mesh_ax)
+    carry, right_arr = (extra, lax.axis_index(mesh_ax))
+    all_values, block_now = (block_in[None], 1)
+    while block_now < carry:
+        buffers = []
+        q = 0
+        while q < carry:
+            buffers.append((q, q ^ block_now))
+            q = q + 1
+        seen_now = lax.ppermute(all_values, axis_name=mesh_ax, perm=buffers)
+        h_now = right_arr & block_now == 0
+        all_values = jnp.concatenate(
+            [jnp.where(h_now, all_values, seen_now), jnp.where(h_now, seen_now, all_values)]
+        )
+        block_now *= 2
+    return all_values
 
 
 def padded_2(array, sides, width):
@@ -69,7 +96,7 @@
         return jnp.einsum("aic,anc->ni", weighted, carried, precision=lax.Precision.HIGHEST)
 
     for repeat in range(STEPS):
-        everyone = lax.all_gather(coeffs, "space", axis=0, tiled=True)
+        everyone = extend_units_in(open_notes(coeffs, "space"), 0)
         rows_each = math.gcd(own_count * lax.axis_size("space"), 128)
         stacked = everyone.reshape(
             own_count * lax.axis_size("space") // rows_each, rows_each, mode_count

time: 244 us -> 234 us (0.959)
  blocking collectives: 35 us -> 0 us
  waiting for transfers between devices: 179 us -> 194 us
  starting transfers between devices: 2.68 us -> 12.8 us
    all_gather x2 -> x0, blocking collectives: 35 us -> none  [shards(): everyone = lax.all_gather(coeffs, 'space', axis=0, tiled=True)]
    ppermute x0 -> x8, waiting for transfers between devices: none -> 14.7 us  [open_notes(): seen_now = lax.ppermute(all_values, axis_name=mesh_ax, perm=buffers)]
    ppermute x0 -> x8, starting transfers between devices: none -> 11.9 us  [open_notes(): seen_now = lax.ppermute(all_values, axis_name=mesh_ax, perm=buffers)]
  transfers between devices with their start and end apart: 4 -> 12, of which waited for: 2 -> 8; matrix products, arithmetic and copies ran while one was open for 1% -> 1% of each run, Pallas kernels for 0% -> 0%
where the time goes in v1:
time: 234 us
  waiting for transfers between devices  194 us (83%)
  between operations  14.3 us (6%)
  starting transfers between devices  12.8 us (5%)
  matrix products  8.41 us (4%)
  local copies, waits for them, and re-layouts  3.41 us (1%)
    psum x1, waiting for transfers between devices, shards(): lax.psum(jnp.einsum('taic,tajc->ij', slopes * cell_scale[None, None, None...  91.9 us
    unnamed x3, waiting for transfers between devices  87.9 us
    ppermute x8, waiting for transfers between devices, open_notes(): seen_now = lax.ppermute(all_values, axis_name=mesh_ax, perm=buffers)  14.7 us
    ppermute x8, starting transfers between devices, open_notes(): seen_now = lax.ppermute(all_values, axis_name=mesh_ax, perm=buffers)  11.9 us
  transfers between devices with their start and end apart: 12, of which 8 were waited for; matrix products, arithmetic and copies ran while one was open for 1% of the time, Pallas kernels for 0%

profile of v1, /device:TPU:8, one launch (start us, length us, event | category | flops | bytes accessed | tf_op | source)
XLA Modules:
  0.0 233.6 jit_solution(4883397263140988671)
XLA Ops:
  6.5 0.8 collective-permute-start.1
  7.4 0.8 fusion.34
  8.3 0.8 collective-permute-start.2
  9.1 0.9 copy-done.3
  10.2 2.4 %collective-permute-start.3 = (f32[2,8,128]{2,1,0:T(8,128)S(1)}, f32[2,8,128]{2,1,0:T(8,128)S(1)}, u32[]{:S(2)}, u32[]{:S(2)}) collective-permute-start(f32[2,8,128]{2,1,0:T(8,128)S(1)} %pad_maximum_fusion.13), channel_id=1, source_target_pairs={{0,2},{1,3},{2,0},{3,1},{4,6},{5,7},{6,4},{7,5},{8,10},{9,11},{10,... | collective-permute-start | bytes 24584 | tf_op jit(solution)/shard_map/ppermute | solution.py:29
  12.6 1.6 collective-permute-done.3
  14.3 2.5 %collective-permute-start.4 = (f32[4,8,128]{2,1,0:T(8,128)S(1)}, f32[4,8,128]{2,1,0:T(8,128)S(1)}, u32[]{:S(2)}, u32[]{:S(2)}) collective-permute-start(f32[4,8,128]{2,1,0:T(8,128)S(1)} %pad_maximum_fusion.11), channel_id=1, source_target_pairs={{0,4},{1,5},{2,6},{3,7},{4,0},{5,1},{6,2},{7,3},{8,12},{9,13},{10,... | collective-permute-start | bytes 49160 | tf_op jit(solution)/shard_map/ppermute | solution.py:29
  16.8 1.7 collective-permute-done.4
  18.5 4.0 %collective-permute-start.5 = (f32[8,8,128]{2,1,0:T(8,128)S(1)}, f32[8,8,128]{2,1,0:T(8,128)S(1)}, u32[]{:S(2)}, u32[]{:S(2)}) collective-permute-start(f32[8,8,128]{2,1,0:T(8,128)S(1)} %pad_maximum_fusion.9), channel_id=1, source_target_pairs={{0,8},{1,9},{2,10},{3,11},{4,12},{5,13},{6,14},{7,15},{8,0},{9,1},... | collective-permute-start | bytes 98312 | tf_op jit(solution)/shard_map/ppermute | solution.py:29
  22.9 0.6 copy-done.7
  25.4 1.0 convolution_bitcast_fusion.6
  27.0 1.0 convolution_bitcast_fusion.5
  28.1 0.6 copy-done.6
  28.9 91.9 %all-reduce.8.cloned.1.call-done = (f32[128,128]{1,0:T(8,128)}, f32[128,128]{1,0:T(8,128)}) async-done(((f32[128,128]{1,0:T(8,128)}, f32[128,128]{1,0:T(8,128)}), (f32[128,128]{1,0:T(8,128)}, f32[128,128]{1,0:T(8,128)})) %all-reduce.8.cloned.1.call-update) | async-done | bytes 131088 | tf_op jit(solution)/shard_map/psum | solution.py:75
  120.8 1.0 fusion.11
  121.8 1.2 collective-permute-done.6
  123.6 3.1 %collective-permute-done.7 = f32[2,8,128]{2,1,0:T(8,128)S(1)} collective-permute-done((f32[2,8,128]{2,1,0:T(8,128)S(1)}, f32[2,8,128]{2,1,0:T(8,128)S(1)}, u32[]{:S(2)}, u32[]{:S(2)}) %collective-permute-start.7) | collective-permute-done | bytes 8224 | tf_op jit(solution)/shard_map/ppermute | solution.py:29
  126.7 3.7 %collective-permute-done.8 = f32[4,8,128]{2,1,0:T(8,128)S(1)} collective-permute-done((f32[4,8,128]{2,1,0:T(8,128)S(1)}, f32[4,8,128]{2,1,0:T(8,128)S(1)}, u32[]{:S(2)}, u32[]{:S(2)}) %collective-permute-start.8) | collective-permute-done | bytes 16416 | tf_op jit(solution)/shard_map/ppermute | solution.py:29
  130.5 1.5 collective-permute-start.9
  132.0 3.4 %collective-permute-done.9 = f32[8,8,128]{2,1,0:T(8,128)S(1)} collective-permute-done((f32[8,8,128]{2,1,0:T(8,128)S(1)}, f32[8,8,128]{2,1,0:T(8,128)S(1)}, u32[]{:S(2)}, u32[]{:S(2)}) %collective-permute-start.9) | collective-permute-done | bytes 32800 | tf_op jit(solution)/shard_map/ppermute | solution.py:29
  135.7 0.6 fusion.3
  136.3 1.0 convolution_bitcast_fusion.4
  137.4 87.9 %all-reduce.6.cloned.1.call-done = f32[128,128]{1,0:T(8,128)} async-done(((f32[128,128]{1,0:T(8,128)}), f32[128,128]{1,0:T(8,128)}) %all-reduce.6.cloned.1.call-update) | async-done | bytes 65552
  225.3 1.5 fusion.7
  (58 shorter events, 3.8 us)
Async XLA Ops:
  6.5 0.9 copy-start
  6.5 2.5 %copy-start.1 = (f32[2,128,2,64]{1,3,2,0:T(8,128)S(1)}, f32[2,128,2,64]{1,3,2,0:T(8,128)}, u32[]{:S(2)}) copy-start(f32[2,128,2,64]{1,3,2,0:T(8,128)} %param.6) | copy-start | bytes 393220
  6.5 114.2 %all-reduce.8.cloned.1.call-start = ((), (), s32[]{:S(2)}) async-start(), calls=%async_computation.1 | async-start | bytes 262144 | tf_op jit(solution)/shard_map/psum | solution.py:75
  6.5 18.7 %collective-permute-start.1 = (f32[2,128,2,64]{1,3,2,0:T(8,128)}, f32[2,128,2,64]{1,3,2,0:T(8,128)S(1)}, u32[]{:S(2)}, u32[]{:S(2)}) collective-permute-start(f32[2,128,2,64]{1,3,2,0:T(8,128)} %param.6), channel_id=1, source_target_pairs={{1,0},{2,1},{3,2},{4,3},{5,4},{6,5},{7,6},{8,7},{9,8},{10,9},{11,1... | collective-permute-start | bytes 393224 | tf_op jit(solution)/shard_map/ppermute | solution.py:46
  7.4 17.9 %collective-permute-start = (f32[2,128,2,64]{1,3,2,0:T(8,128)}, f32[2,128,2,64]{1,3,2,0:T(8,128)S(1)}, u32[]{:S(2)}, u32[]{:S(2)}) collective-permute-start(f32[2,128,2,64]{1,3,2,0:T(8,128)} %param.6), channel_id=1, source_target_pairs={{0,1},{1,2},{2,3},{3,4},{4,5},{5,6},{6,7},{7,8},{8,9},{9,10},{10,1... | collective-permute-start | bytes 393224 | tf_op jit(solution)/shard_map/ppermute | solution.py:45
  8.3 1.9 collective-permute-start.2
  9.1 0.9 copy-start.3
  9.1 0.9 copy-start.4
  10.2 4.0 %collective-permute-start.3 = (f32[2,8,128]{2,1,0:T(8,128)S(1)}, f32[2,8,128]{2,1,0:T(8,128)S(1)}, u32[]{:S(2)}, u32[]{:S(2)}) collective-permute-start(f32[2,8,128]{2,1,0:T(8,128)S(1)} %pad_maximum_fusion.13), channel_id=1, source_target_pairs={{0,2},{1,3},{2,0},{3,1},{4,6},{5,7},{6,4},{7,5},{8,10},{9,11},{10,... | collective-permute-start | bytes 24584 | tf_op jit(solution)/shard_map/ppermute | solution.py:29
  14.2 2.6 %copy-start.5 = (f32[2,64]{1,0:T(2,128)S(1)}, f32[2,64]{1,0:T(2,128)}, u32[]{:S(2)}) copy-start(f32[2,64]{1,0:T(2,128)} %param.7) | copy-start | bytes 1540
  14.3 4.3 %collective-permute-start.4 = (f32[4,8,128]{2,1,0:T(8,128)S(1)}, f32[4,8,128]{2,1,0:T(8,128)S(1)}, u32[]{:S(2)}, u32[]{:S(2)}) collective-permute-start(f32[4,8,128]{2,1,0:T(8,128)S(1)} %pad_maximum_fusion.11), channel_id=1, source_target_pairs={{0,4},{1,5},{2,6},{3,7},{4,0},{5,1},{6,2},{7,3},{8,12},{9,13},{10,... | collective-permute-start | bytes 49160 | tf_op jit(solution)/shard_map/ppermute | solution.py:29
  18.5 6.3 %collective-permute-start.5 = (f32[8,8,128]{2,1,0:T(8,128)S(1)}, f32[8,8,128]{2,1,0:T(8,128)S(1)}, u32[]{:S(2)}, u32[]{:S(2)}) collective-permute-start(f32[8,8,128]{2,1,0:T(8,128)S(1)} %pad_maximum_fusion.9), channel_id=1, source_target_pairs={{0,8},{1,9},{2,10},{3,11},{4,12},{5,13},{6,14},{7,15},{8,0},{9,1},... | collective-permute-start | bytes 98312 | tf_op jit(solution)/shard_map/ppermute | solution.py:29
  22.9 0.7 copy-start.7
  28.0 0.7 copy-start.6
  28.0 197.3 %all-reduce.6.cloned.1.call-start = ((), (), s32[]{:S(2)}) async-start(), calls=%async_computation | async-start | bytes 131072
  121.8 1.2 collective-permute-start.6
  123.0 3.7 %collective-permute-start.7 = (f32[2,8,128]{2,1,0:T(8,128)S(1)}, f32[2,8,128]{2,1,0:T(8,128)S(1)}, u32[]{:S(2)}, u32[]{:S(2)}) collective-permute-start(f32[2,8,128]{2,1,0:T(8,128)S(1)} %pad_maximum_fusion.14), channel_id=1, source_target_pairs={{0,2},{1,3},{2,0},{3,1},{4,6},{5,7},{6,4},{7,5},{8,10},{9,11},{10,... | collective-permute-start | bytes 24584 | tf_op jit(solution)/shard_map/ppermute | solution.py:29
  126.7 3.8 %collective-permute-start.8 = (f32[4,8,128]{2,1,0:T(8,128)S(1)}, f32[4,8,128]{2,1,0:T(8,128)S(1)}, u32[]{:S(2)}, u32[]{:S(2)}) collective-permute-start(f32[4,8,128]{2,1,0:T(8,128)S(1)} %pad_maximum_fusion.12), channel_id=1, source_target_pairs={{0,4},{1,5},{2,6},{3,7},{4,0},{5,1},{6,2},{7,3},{8,12},{9,13},{10,... | collective-permute-start | bytes 49160 | tf_op jit(solution)/shard_map/ppermute | solution.py:29
  130.5 4.9 %collective-permute-start.9 = (f32[8,8,128]{2,1,0:T(8,128)S(1)}, f32[8,8,128]{2,1,0:T(8,128)S(1)}, u32[]{:S(2)}, u32[]{:S(2)}) collective-permute-start(f32[8,8,128]{2,1,0:T(8,128)S(1)} %pad_maximum_fusion.10), channel_id=1, source_target_pairs={{0,8},{1,9},{2,10},{3,11},{4,12},{5,13},{6,14},{7,15},{8,0},{9,1},... | collective-permute-start | bytes 98312 | tf_op jit(solution)/shard_map/ppermute | solution.py:29
  137.4 87.9 %copy-start.2 = (f32[128,128]{1,0:T(8,128)S(1)}, f32[128,128]{1,0:T(8,128)}, u32[]{:S(2)}) copy-start(f32[128,128]{1,0:T(8,128)} %get-tuple-element.27) | copy-start | bytes 196612
Sparse Core Ops, SparseCore 0:
  28.1 92.6 all-reduce.7
  137.5 87.7 all-reduce.5
